TPU v7x, 128 devices: a whole 4x4x4 slice. The times are simulated.
128 devices in a mesh: req: 32 (over x, y, core), mlp: 4 (over z).
Axes of the slice: x: 4, y: 4, z: 4, core: 2. Of those that a mesh axis runs over, the one named last changes fastest.
Arguments:
- hidden_in: bfloat16 [64, 512, 2048], P('req'), may hold values from -6 to 6
- lengths: int32 [64], replicated, may hold values from 1 to 512, 16384 in all
- slot_request: int32 [64], replicated, may hold values from 0 to 63, each once
- adapter_of: int32 [64], replicated, may hold values from 0 to 63, as said below
- adapter_slot: int32 [64], replicated, may hold values from 0 to 63, each once
- norm_gain_attn: float32 [2048], replicated, may hold values from 0.5 to 1.5
- norm_gain_mlp: float32 [2048], replicated, may hold values from 0.5 to 1.5
- final_gain: float32 [2048], replicated, may hold values from 0.5 to 1.5
- w_qkv: bfloat16 [2048, 3, 2048], P(None, None, 'mlp')
- w_out: bfloat16 [2048, 2048], P('mlp'), may hold values from -0.125 to 0.125
- w_gateup: bfloat16 [2048, 2, 4096], P('req', None, 'mlp'), may hold values from -0.125 to 0.125
- w_down: bfloat16 [4096, 2048], P('mlp', 'req'), may hold values from -0.09375 to 0.09375
- adapter_down: bfloat16 [64, 16, 2048], P('req'), may hold values from -0.125 to 0.125
- adapter_up: bfloat16 [64, 16, 2048], P('req', None, 'mlp'), may hold values from -1.5 to 1.5
- vocab: bfloat16 [49152, 2048], P(('req', 'mlp')), may hold values from -0.375 to 0.375
Outputs:
- out_hidden: bfloat16 [64, 512, 2048], P('req')
- request_norm: float32 [64], replicated
- request_peak: float32 [64], replicated
Inputs may be any that keep to these rules, and one draw needn't show every extreme that they name: Some request has exactly 512 tokens, and all lengths together sum to 16384. `slot_request`: each request sits in exactly one slot. `adapter_of`: exactly 16 distinct adapters are named. `adapter_slot`: each adapter sits in exactly one row of the adapter tables.
All inputs are finite; a program needn't handle non-finite values.
Results may differ from a plain program's by a relative error of at most 0.018.
Values may be sent and summed in bfloat16 or wider, within the bound.
A program may use at most 128 MiB of HBM per device.

v0:
```python
import jax
import jax.numpy as jnp
from jax import lax
from jax.sharding import PartitionSpec as P

HEAD_WIDTH = 64
EPSILON = 1e-05
ROPE_BASE = 130000.0
ADAPTER_SCALE = 2.0
MASKED = -1e30


def rms_norm(values, gain):
    return values * lax.rsqrt(jnp.mean(values * values, axis=-1, keepdims=True) + EPSILON) * gain


def rotary_embedded(tensor):
    length = tensor.shape[-3]
    half_width = tensor.shape[-1] // 2
    frequency = ROPE_BASE ** (-(jnp.arange(half_width, dtype=jnp.float32) * 2.0 / tensor.shape[-1]))
    angles = jnp.arange(length, dtype=jnp.float32)[:, None] * frequency[None, :]
    cosine = jnp.cos(angles)[:, None, :]
    sine_part = jnp.sin(angles)[:, None, :]
    front_half = tensor[..., :half_width]
    back_half = tensor[..., half_width:]
    return jnp.concatenate(
        [front_half * cosine - back_half * sine_part, back_half * cosine + front_half * sine_part],
        axis=-1,
    )


def per_device(
    hidden_in,
    lengths,
    slot_request,
    adapter_of,
    adapter_slot,
    norm_gain_attn,
    norm_gain_mlp,
    final_gain,
    w_qkv,
    w_out,
    w_gateup,
    w_down,
    adapter_down,
    adapter_up,
    vocab,
):
    req_index = lax.axis_index("req")
    slots_number, sequence_length, width = hidden_in.shape
    row_count = slots_number * sequence_length
    head_cols = w_qkv.shape[2]
    heads_number = head_cols // HEAD_WIDTH
    unit_cols = w_gateup.shape[2]
    requests = lax.dynamic_slice_in_dim(slot_request, req_index * slots_number, slots_number)
    own_lengths = jnp.take(lengths, requests)
    own_adapters = jnp.take(adapter_of, requests)
    table_rows = jnp.take(adapter_slot, own_adapters)
    positions = jnp.arange(sequence_length, dtype=jnp.int32)
    residual_in = hidden_in.astype(jnp.float32)
    normed = rms_norm(residual_in, norm_gain_attn).astype(jnp.bfloat16)
    projected_rows = jnp.dot(
        normed.reshape(row_count, width),
        w_qkv.reshape(width, 3 * head_cols),
        preferred_element_type=jnp.float32,
    ).reshape(slots_number, sequence_length, 3, head_cols)
    down_all, up_all = (
        lax.all_gather(adapter_down, "req", axis=0, tiled=True),
        lax.all_gather(adapter_up, "req", axis=0, tiled=True),
    )
    down_rows = jnp.take(down_all, table_rows, axis=0)
    up_rows = jnp.take(up_all, table_rows, axis=0)
    low_rank = jnp.einsum(
        "bsd,brd->bsr", normed, down_rows, preferred_element_type=jnp.float32
    ).astype(jnp.bfloat16)
    raised_rows = jnp.einsum("bsr,brc->bsc", low_rank, up_rows, preferred_element_type=jnp.float32)
    queries = rotary_embedded(
        (projected_rows[:, :, 0] + ADAPTER_SCALE * raised_rows).reshape(
            slots_number, sequence_length, heads_number, HEAD_WIDTH
        )
    ).astype(jnp.bfloat16)
    key_heads = rotary_embedded(
        projected_rows[:, :, 1].reshape(slots_number, sequence_length, heads_number, HEAD_WIDTH)
    ).astype(jnp.bfloat16)
    value_heads = (
        projected_rows[:, :, 2]
        .reshape(slots_number, sequence_length, heads_number, HEAD_WIDTH)
        .astype(jnp.bfloat16)
    )
    causal = positions[None, :] <= positions[:, None]

    def attend(slot_items):
        query_one, key_one, value_one, length = slot_items
        scores = jnp.einsum(
            "qhd,khd->hqk", query_one, key_one, preferred_element_type=jnp.float32
        ) * HEAD_WIDTH ** (-0.5)
        allowed = causal & (positions[None, :] < length)
        scores = jnp.where(allowed[None], scores, MASKED)
        probabilities = jax.nn.softmax(scores, axis=-1).astype(jnp.bfloat16)
        return jnp.einsum(
            "hqk,khd->qhd", probabilities, value_one, preferred_element_type=jnp.float32
        ).astype(jnp.bfloat16)

    attended = lax.map(attend, (queries, key_heads, value_heads, own_lengths))
    head_part = jnp.dot(
        attended.reshape(row_count, head_cols), w_out, preferred_element_type=jnp.float32
    )
    mixed_heads = lax.psum(head_part.astype(jnp.bfloat16), "mlp").astype(jnp.float32)
    stream = (residual_in + mixed_heads.reshape(slots_number, sequence_length, width)).astype(
        jnp.bfloat16
    )
    normed_mid = (
        rms_norm(stream.astype(jnp.float32), norm_gain_mlp)
        .astype(jnp.bfloat16)
        .reshape(row_count, width)
    )
    shard_piece = lax.all_gather(w_gateup, "req", axis=0, tiled=True)
    gate_up = jnp.dot(
        normed_mid,
        shard_piece.reshape(shard_piece.shape[0], 2 * unit_cols),
        preferred_element_type=jnp.float32,
    )
    activated = (jax.nn.silu(gate_up[:, :unit_cols]) * gate_up[:, unit_cols:]).astype(jnp.bfloat16)
    unit_part = jnp.dot(
        activated,
        lax.all_gather(w_down, "req", axis=1, tiled=True),
        preferred_element_type=jnp.float32,
    )
    unit_total = lax.psum(unit_part.astype(jnp.bfloat16), "mlp").astype(jnp.float32)
    result = stream.astype(jnp.float32) + unit_total.reshape(slots_number, sequence_length, width)
    live = positions[None, :] < own_lengths[:, None]
    out_hidden = jnp.where(live[:, :, None], result, 0.0).astype(jnp.bfloat16)
    out_float = out_hidden.astype(jnp.float32)
    square_sum = jnp.sum(out_float * out_float, axis=(1, 2))
    slot_norm = jnp.sqrt(square_sum / (own_lengths.astype(jnp.float32) * width))
    picked = (positions[None, :] == own_lengths[:, None] - 1).astype(jnp.float32)
    last_rows = jnp.einsum("bs,bsd->bd", picked, out_float, precision=lax.Precision.HIGHEST)
    last_rounded = lax.optimization_barrier(rms_norm(last_rows, final_gain).astype(jnp.bfloat16))
    last_normed = last_rounded.astype(jnp.float32)
    every_last, every_norm = (
        lax.all_gather(last_normed, "req", axis=0, tiled=True),
        lax.all_gather(slot_norm, "req", axis=0, tiled=True),
    )
    logits = lax.dot_general(
        every_last.astype(jnp.bfloat16),
        vocab,
        (((1,), (1,)), ((), ())),
        preferred_element_type=jnp.float32,
    )
    slot_peak = lax.pmax(jnp.max(logits, axis=1), ("req", "mlp"))
    request_total = slot_request.shape[0]
    owners = slot_request[None, :] == jnp.arange(request_total, dtype=jnp.int32)[:, None]
    request_norm = jnp.sum(jnp.where(owners, every_norm[None, :], 0.0), axis=1)
    request_peak = jnp.sum(jnp.where(owners, slot_peak[None, :], 0.0), axis=1)
    return (out_hidden, request_norm, request_peak)


def solution(mesh):
    return jax.shard_map(
        per_device,
        mesh=mesh,
        in_specs=(
            P("req", None, None),
            P(),
            P(),
            P(),
            P(),
            P(),
            P(),
            P(),
            P(None, None, "mlp"),
            P("mlp", None),
            P("req", None, "mlp"),
            P("mlp", "req"),
            P("req", None, None),
            P("req", None, "mlp"),
            P(("req", "mlp"), None),
        ),
        out_specs=(P("req", None, None), P(), P()),
        check_vma=False,
    )
```

profile of v0, /device:TPU:0, one launch (start us, length us, event | category | flops | bytes accessed | tf_op | source)
XLA Modules:
  0.0 623.8 jit_solution(15625885839021791205)
XLA Ops:
  8.7 8.8 %copy.26 = bf16[2048,3,512]{0,2,1:T(8,128)(2,1)} copy(bf16[2048,3,512]{2,0,1:T(8,128)(2,1)} %param.27) | data formatting | bytes 12582912 | tf_op args[8]
  21.0 9.1 %fusion.53 = f32[2,512,3,512]{1,3,2,0:T(8,128)S(1)} fusion(bf16[2048,3,512]{0,2,1:T(8,128)(2,1)} %copy.26, bf16[2,512,2048]{2,1,0:T(8,128)(2,1)S(1)} %copy-done.4, f32[2048]{0:T(1024)S(1)} %copy-done.13, f32[2,512]{1,0:T(2,128)S(1)} %add_rsqrt_fusion.1), kind=kOutput, calls=%fused_computation.55 | convolution fusion | flops 6450839552 | bytes 16789504 | tf_op jit(solution)/shard_map/dot_general | solution.py:62
  36.0 19.5 %all-gather.8.cloned.1.call-done = bf16[64,16,512]{2,1,0:T(8,128)(2,1)} async-done(((bf16[2,16,512]{2,1,0:T(8,128)(2,1)}), bf16[64,16,512]{2,1,0:T(8,128)(2,1)}) %all-gather.8.cloned.1.call-update) | async-done | bytes 1048592 | tf_op jit(solution)/shard_map/all_gather | solution.py:69
  57.2 45.8 %all-gather.6.cloned.1.call-done = bf16[64,16,2048]{2,1,0:T(8,128)(2,1)} async-done(((bf16[2,16,2048]{2,1,0:T(8,128)(2,1)}), bf16[64,16,2048]{2,1,0:T(8,128)(2,1)}) %all-gather.6.cloned.1.call-update) | async-done | bytes 4194320 | tf_op jit(solution)/shard_map/all_gather | solution.py:68
  105.8 5.8 fusion.61
  116.0 28.0 %while.11 = (s32[]{:T(128)}, bf16[2,512,8,64]{1,3,2,0:T(8,128)(2,1)}, bf16[2,512,8,64]{1,3,2,0:T(8,128)(2,1)S(1)}, s32[2]{0:T(128)S(1)}, bf16[2,512,8,64]{1,3,2,...) while((s32[]{:T(128)}, bf16[2,512,8,64]{1,3,2,0:T(8,128)(2,1)}, ...), condition=%wide.region_4.6_spmd.clone, body=%wide.region_1.5_spmd.clone.sunk | while | flops 550241280 | bytes 19434588 | solution.py:104
  117.3 7.6 %fusion.116 = (f32[8,512]{1,0:T(8,128)S(1)}, f32[8,512,512]{1,2,0:T(8,128)}) fusion(pred[512,512]{0,1:T(8,128)(4,1)S(1)} %fusion.115, bf16[2,512,8,64]{1,3,2,0:T(8,128)(2,1)} %get-tuple-element.155, s32[]{:T(128)} %get-tuple-element.143, bf16[2,512,8,64]{1,3,2,0:T(8,128)(2,1)} %get-tuple-element.154), kind=kOutput, calls=%fused_computation.116.clone.1 | convolution fusion | flops 276824576 | bytes 9716736 | tf_op jit(solution)/shard_map/while/body/eval_jaxpr/sub | solution.py:99
  124.9 5.0 fusion.117
  131.3 7.6 %fusion.116 = (f32[8,512]{1,0:T(8,128)S(1)}, f32[8,512,512]{1,2,0:T(8,128)}) fusion(pred[512,512]{0,1:T(8,128)(4,1)S(1)} %fusion.115, bf16[2,512,8,64]{1,3,2,0:T(8,128)(2,1)} %get-tuple-element.155, s32[]{:T(128)} %get-tuple-element.143, bf16[2,512,8,64]{1,3,2,0:T(8,128)(2,1)} %get-tuple-element.154), kind=kOutput, calls=%fused_computation.116.clone.1 | convolution fusion | flops 276824576 | bytes 9716736 | tf_op jit(solution)/shard_map/while/body/eval_jaxpr/sub | solution.py:99
  138.9 5.0 fusion.117
  146.5 4.4 convolution_convert_fusion
  152.2 91.4 %all-reduce.4.cloned.1.call-done = bf16[2,512,2048]{2,1,0:T(8,128)(2,1)} async-done(((bf16[2,512,2048]{2,1,0:T(8,128)(2,1)}), bf16[2,512,2048]{2,1,0:T(8,128)(2,1)}) %all-reduce.4.cloned.1.call-update) | async-done | bytes 4194320 | tf_op jit(solution)/shard_map/psum | solution.py:108
  243.6 5.0 fusion.48
  249.5 3.6 fusion.50
  253.1 45.4 %all-gather.10.cloned.1.call-done = bf16[2048,2,1024]{2,1,0:T(2,128)(2,1)} async-done(((bf16[64,2,1024]{2,1,0:T(2,128)(2,1)}), bf16[2048,2,1024]{2,1,0:T(2,128)(2,1)}) %all-gather.10.cloned.1.call-update) | async-done | bytes 8388624 | tf_op jit(solution)/shard_map/all_gather | solution.py:117
  298.5 10.3 %copy.33 = bf16[256,8,2,1024]{3,1,2,0:T(8,128)(2,1)} copy(bf16[256,8,2,1024]{3,2,1,0:T(2,128)(2,1)} %bitcast.100) | data formatting | bytes 16777216
  308.8 13.3 %fusion.97 = f32[1024,2048]{1,0:T(8,128)} fusion(bf16[1024,2048]{1,0:T(8,128)(2,1)S(1)} %bitcast.102, bf16[2048,2048]{1,0:T(8,128)(2,1)} %bitcast.101), kind=kOutput, calls=%fused_computation.117 | convolution fusion | flops 8589934592 | bytes 20971520 | tf_op jit(solution)/shard_map/dot_general | solution.py:118
  322.0 24.4 %all-gather.12.cloned.1.call-done = bf16[1024,2048]{0,1:T(8,128)(2,1)} async-done(((bf16[1024,64]{0,1:T(8,128)(2,1)}), bf16[1024,2048]{0,1:T(8,128)(2,1)}) %all-gather.12.cloned.1.call-update) | async-done | bytes 4194320 | tf_op jit(solution)/shard_map/all_gather | solution.py:126
  346.4 11.2 %convolution_convert_fusion.1 = bf16[1024,2048]{1,0:T(8,128)(2,1)} fusion(bf16[1024,2048]{0,1:T(8,128)(2,1)} %all-gather.12.cloned.1.call-done, f32[1024,2048]{1,0:T(8,128)} %fusion.97), kind=kOutput, calls=%fused_computation.61 | convolution fusion | flops 4303355904 | bytes 16777216 | tf_op jit(solution)/shard_map/dot_general | solution.py:124
  359.7 90.6 %all-reduce.6.cloned.1.call-done = bf16[2,512,2048]{2,1,0:T(8,128)(2,1)} async-done(((bf16[2,512,2048]{2,1,0:T(8,128)(2,1)}), bf16[2,512,2048]{2,1,0:T(8,128)(2,1)}) %all-reduce.6.cloned.1.call-update) | async-done | bytes 4194320 | tf_op jit(solution)/shard_map/psum | solution.py:129
  450.3 6.9 %multiply_reduce_fusion = (f32[2]{0:T(128)S(1)}, bf16[2,512,2048]{2,1,0:T(8,128)(2,1)S(1)}) fusion(bf16[2,512,2048]{2,1,0:T(8,128)(2,1)} %all-reduce.6.cloned.1.call-done, bf16[2,512,2048]{2,1,0:T(8,128)(2,1)} %all-reduce.4.cloned.1.call-done, bf16[2,512,2048]{2,1,0:T(8,128)(2,1)} %param.19, pred[2,512]{1,0:T(4,128)(4,1)S(1)} %iota_compare_fusion.3), kind=kLoop, calls=%fused_computation.54 | loop fusion | flops 25165822 | bytes 16778248 | tf_op jit(solution)/shard_map/reduce_sum | solution.py:134
  460.2 24.8 %all-gather = bf16[32,2,2048]{2,1,0:T(2,128)(2,1)S(1)} all-gather(bf16[1,2,2048]{2,1,0:T(2,128)(2,1)S(1)} %bitcast.109), channel_id=1, replica_groups=mesh['req'=32,'mlp'=4] {'req'}, dimensions={0}, use_global_device_ids=true | all-gather | bytes 270336 | tf_op jit(solution)/shard_map/all_gather | solution.py:141
  487.2 64.5 %pmax.7 = f32[64]{0:T(128)S(1)} all-reduce(f32[64]{0:T(128)S(1)} %convolution_reduce_fusion), channel_id=1, replica_groups=mesh['req'=32,'mlp'=4] {'req','mlp'}, use_global_device_ids=true, to_apply=%region_12.14 | all-reduce | flops 64 | bytes 512 | tf_op jit(solution)/shard_map/pmax | solution.py:150
  551.7 64.6 %all-reduce = f32[64]{0:T(128)S(1)} all-reduce(f32[64]{0:T(128)S(1)} %sqrt_dynamic-update-slice_fusion), channel_id=1, replica_groups=mesh['req'=32,'mlp'=4] {'req'}, use_global_device_ids=true, to_apply=%add | all-reduce | flops 64 | bytes 512
  (83 shorter events, 34.2 us)
Async XLA Ops:
  7.2 139.3 %copy-start = (bf16[512,2048]{1,0:T(8,128)(2,1)S(1)}, bf16[512,2048]{1,0:T(8,128)(2,1)}, u32[]{:S(2)}) copy-start(bf16[512,2048]{1,0:T(8,128)(2,1)} %param.28) | copy-start | bytes 6291460
  7.2 48.2 %all-gather.8.cloned.1.call-start = ((), (), s32[]{:S(2)}) async-start(), calls=%async_computation.1 | async-start | bytes 1081344 | tf_op jit(solution)/shard_map/all_gather | solution.py:69
  7.9 95.1 %all-gather.6.cloned.1.call-start = ((), (), s32[]{:S(2)}) async-start(), calls=%async_computation | async-start | bytes 4325376 | tf_op jit(solution)/shard_map/all_gather | solution.py:68
  8.7 234.9 %all-reduce.4.cloned.1.call-start = ((), (), s32[]{:S(2)}) async-start(), calls=%async_computation.2 | async-start | bytes 8388608 | tf_op jit(solution)/shard_map/psum | solution.py:108
  17.5 3.4 copy-start.4
  17.5 3.4 copy-start.13
  30.1 3.3 copy-start.9
  30.1 3.4 copy-start.12
  30.1 3.5 copy-start.1
  30.1 4.1 copy-start.2
  30.1 4.9 copy-start.3
  150.9 147.5 %all-gather.10.cloned.1.call-start = ((), (), s32[]{:S(2)}) async-start(), calls=%async_computation.3 | async-start | bytes 8650752 | tf_op jit(solution)/shard_map/all_gather | solution.py:117
  151.5 194.9 %all-gather.12.cloned.1.call-start = ((), (), s32[]{:S(2)}) async-start(), calls=%async_computation.4 | async-start | bytes 4325376 | tf_op jit(solution)/shard_map/all_gather | solution.py:126
  152.1 96.5 %copy-start.10 = (f32[2048]{0:T(1024)S(1)}, f32[2048]{0:T(1024)}, u32[]{:S(2)}) copy-start(f32[2048]{0:T(1024)} %param.25) | copy-start | bytes 24580
  152.1 298.2 %all-reduce.6.cloned.1.call-start = ((), (), s32[]{:S(2)}) async-start(), calls=%async_computation.5 | async-start | bytes 8388608 | tf_op jit(solution)/shard_map/psum | solution.py:129
  243.6 5.1 copy-start.5
  243.6 5.9 copy-start.6
  298.5 10.3 %copy-start.8 = (bf16[2,512,2048]{2,1,0:T(8,128)(2,1)S(1)}, bf16[2,512,2048]{2,1,0:T(8,128)(2,1)}, u32[]{:S(2)}) copy-start(bf16[2,512,2048]{2,1,0:T(8,128)(2,1)} %fusion.50) | copy-start | bytes 12582916
  357.6 0.7 copy-start.14
  457.3 2.0 copy-start.7
  457.3 2.8 copy-start.11
Sparse Core Ops, SparseCore 0:
  10.3 45.0 all-gather.7
  57.7 45.2 all-gather.5
  151.1 92.4 all-reduce.3
  246.0 52.4 all-gather.9
  300.8 45.5 all-gather.11
  357.8 92.4 all-reduce.5
where the time goes:
time: 624 us
  waiting for transfers between devices  320 us (51%)
  blocking collectives  154 us (25%)
  matrix products  71.7 us (11%)
  local copies, waits for them, and re-layouts  37.1 us (6%)
  other arithmetic  26.4 us (4%)
  between operations  15 us (2%)
    psum x1, waiting for transfers between devices, per_device(): lax.psum(head_part.astype(jnp.bfloat16), 'mlp').astype(jnp.float32)  91.4 us
    psum x1, waiting for transfers between devices, per_device(): lax.psum(unit_part.astype(jnp.bfloat16), 'mlp').astype(jnp.float32)  90.6 us
    unnamed x1, blocking collectives  64.6 us
    pmax x1, blocking collectives, per_device(): slot_peak = lax.pmax(jnp.max(logits, axis=1), ('req', 'mlp'))  64.5 us
    all_gather x1, waiting for transfers between devices, per_device(): lax.all_gather(adapter_down, 'req', axis=0, tiled=True)  45.8 us
    all_gather x1, waiting for transfers between devices, per_device(): shard_piece = lax.all_gather(w_gateup, 'req', axis=0, tiled=True)  45.4 us
    unnamed x35, local copies, waits for them, and re-layouts  25.3 us
    all_gather x1, blocking collectives, per_device(): lax.all_gather(last_normed, 'req', axis=0, tiled=True)  24.8 us
  transfers between devices with their start and end apart: 6, of which 6 were waited for; matrix products, arithmetic and copies ran while one was open for 10% of the time, Pallas kernels for 0%

commit v1 on v0

--- a/solution.py
+++ b/solution.py
@@ -1,3 +1,4 @@
+import functools
 import jax
 import jax.numpy as jnp
 from jax import lax
@@ -8,6 +9,13 @@
 ROPE_BASE = 130000.0
 ADAPTER_SCALE = 2.0
 MASKED = -1e30
+
+
+def edge_recast(x_local, group_axis):
+    return lax.all_gather(x_local, group_axis).sum(axis=0)
+
+
+try_all_page_now = functools.partial(edge_recast, group_axis="mlp")
 
 
 def rms_norm(values, gain):
@@ -105,7 +113,7 @@
     head_part = jnp.dot(
         attended.reshape(row_count, head_cols), w_out, preferred_element_type=jnp.float32
     )
-    mixed_heads = lax.psum(head_part.astype(jnp.bfloat16), "mlp").astype(jnp.float32)
+    mixed_heads = try_all_page_now(head_part.astype(jnp.bfloat16)).astype(jnp.float32)
     stream = (residual_in + mixed_heads.reshape(slots_number, sequence_length, width)).astype(
         jnp.bfloat16
     )

time: 624 us -> 647 us (1.037); the launches traced: 624 us -> 639 us
  other arithmetic: 26.4 us -> 38.1 us
    all_gather x0 -> x1, waiting for transfers between devices: none -> 146 us  [edge_recast(): return lax.all_gather(x_local, group_axis).sum(axis=0)]
    psum x1 -> x0, waiting for transfers between devices: 91.4 us -> none  [per_device(): lax.psum(head_part.astype(jnp.bfloat16), 'mlp').astype(jnp.float32)]
    all_gather x1, waiting for transfers between devices: 45.4 us -> 5.25 us  [per_device(): shard_piece = lax.all_gather(w_gateup, 'req', axis=0, tiled=True)]
    reduce_sum x0 -> x1, other arithmetic: none -> 12.3 us  [edge_recast(): return lax.all_gather(x_local, group_axis).sum(axis=0)]
    all_gather x1, waiting for transfers between devices: 24.4 us -> 16.4 us  [per_device(): lax.all_gather(w_down, 'req', axis=1, tiled=True)]
    unnamed x35 -> x37, local copies, waits for them, and re-layouts: 25.3 us -> 24.3 us
  transfers between devices with their start and end apart: 6 -> 6, of which waited for: 6 -> 6; matrix products, arithmetic and copies ran while one was open for 10% -> 18% of each run, Pallas kernels for 0% -> 0%
where the time goes in v1:
time: 647 us; the launch traced here: 639 us
  waiting for transfers between devices  325 us (50%)
  blocking collectives  154 us (24%)
  matrix products  69.6 us (11%)
  other arithmetic  38.1 us (6%)
  local copies, waits for them, and re-layouts  36.1 us (6%)
  between operations  15.2 us (2%)
    all_gather x1, waiting for transfers between devices, edge_recast(): return lax.all_gather(x_local, group_axis).sum(axis=0)  146 us
    psum x1, waiting for transfers between devices, per_device(): lax.psum(unit_part.astype(jnp.bfloat16), 'mlp').astype(jnp.float32)  90.7 us
    unnamed x1, blocking collectives  64.6 us
    pmax x1, blocking collectives, per_device(): slot_peak = lax.pmax(jnp.max(logits, axis=1), ('req', 'mlp'))  64.5 us
    all_gather x1, waiting for transfers between devices, per_device(): lax.all_gather(adapter_down, 'req', axis=0, tiled=True)  45.8 us
    all_gather x1, blocking collectives, per_device(): lax.all_gather(last_normed, 'req', axis=0, tiled=True)  24.8 us
    unnamed x37, local copies, waits for them, and re-layouts  24.3 us
    all_gather x1, waiting for transfers between devices, per_device(): lax.all_gather(adapter_up, 'req', axis=0, tiled=True)  18.7 us
  transfers between devices with their start and end apart: 6, of which 6 were waited for; matrix products, arithmetic and copies ran while one was open for 18% of the time, Pallas kernels for 0%

profile of v1, /device:TPU:0, one launch (start us, length us, event | category | flops | bytes accessed | tf_op | source)
XLA Modules:
  0.0 638.8 jit_solution(17526789442634656808)
XLA Ops:
  9.4 8.8 %copy.26 = bf16[2048,3,512]{0,2,1:T(8,128)(2,1)} copy(bf16[2048,3,512]{2,0,1:T(8,128)(2,1)} %param.27) | data formatting | bytes 12582912 | tf_op args[8]
  21.7 9.1 %fusion.53 = f32[2,512,3,512]{1,3,2,0:T(8,128)S(1)} fusion(bf16[2048,3,512]{0,2,1:T(8,128)(2,1)} %copy.26, bf16[2,512,2048]{2,1,0:T(8,128)(2,1)S(1)} %copy-done.5, f32[2048]{0:T(1024)S(1)} %copy-done.14, f32[2,512]{1,0:T(2,128)S(1)} %add_rsqrt_fusion.1), kind=kOutput, calls=%fused_computation.55 | convolution fusion | flops 6450839552 | bytes 16789504 | tf_op jit(solution)/shard_map/dot_general | solution.py:70
  36.7 18.7 %all-gather.10.cloned.1.call-done = bf16[64,16,512]{2,1,0:T(8,128)(2,1)} async-done(((bf16[2,16,512]{2,1,0:T(8,128)(2,1)}), bf16[64,16,512]{2,1,0:T(8,128)(2,1)}) %all-gather.10.cloned.1.call-update) | async-done | bytes 1048592 | tf_op jit(solution)/shard_map/all_gather | solution.py:77
  57.2 45.8 %all-gather.8.cloned.1.call-done = bf16[64,16,2048]{2,1,0:T(8,128)(2,1)} async-done(((bf16[2,16,2048]{2,1,0:T(8,128)(2,1)}), bf16[64,16,2048]{2,1,0:T(8,128)(2,1)}) %all-gather.8.cloned.1.call-update) | async-done | bytes 4194320 | tf_op jit(solution)/shard_map/all_gather | solution.py:76
  105.8 5.8 fusion.61
  116.0 28.6 %while.11 = (s32[]{:T(128)}, bf16[2,512,8,64]{1,3,2,0:T(8,128)(2,1)}, bf16[2,512,8,64]{1,3,2,0:T(8,128)(2,1)S(1)}, s32[2]{0:T(128)S(1)}, bf16[2,512,8,64]{1,3,2,...) while((s32[]{:T(128)}, bf16[2,512,8,64]{1,3,2,0:T(8,128)(2,1)}, ...), condition=%wide.region_4.6_spmd.clone, body=%wide.region_1.5_spmd.clone.sunk | while | flops 550241280 | bytes 19434588 | solution.py:112
  117.3 7.6 %fusion.115 = (f32[8,512]{1,0:T(8,128)S(1)}, f32[8,512,512]{1,2,0:T(8,128)}) fusion(pred[512,512]{0,1:T(8,128)(4,1)S(1)} %fusion.114, bf16[2,512,8,64]{1,3,2,0:T(8,128)(2,1)} %get-tuple-element.153, s32[]{:T(128)} %get-tuple-element.141, bf16[2,512,8,64]{1,3,2,0:T(8,128)(2,1)} %get-tuple-element.152), kind=kOutput, calls=%fused_computation.116.clone.1 | convolution fusion | flops 276824576 | bytes 9716736 | tf_op jit(solution)/shard_map/while/body/eval_jaxpr/sub | solution.py:107
  124.9 5.1 fusion.116
  131.4 7.6 %fusion.115 = (f32[8,512]{1,0:T(8,128)S(1)}, f32[8,512,512]{1,2,0:T(8,128)}) fusion(pred[512,512]{0,1:T(8,128)(4,1)S(1)} %fusion.114, bf16[2,512,8,64]{1,3,2,0:T(8,128)(2,1)} %get-tuple-element.153, s32[]{:T(128)} %get-tuple-element.141, bf16[2,512,8,64]{1,3,2,0:T(8,128)(2,1)} %get-tuple-element.152), kind=kOutput, calls=%fused_computation.116.clone.1 | convolution fusion | flops 276824576 | bytes 9716736 | tf_op jit(solution)/shard_map/while/body/eval_jaxpr/sub | solution.py:107
  139.0 5.2 fusion.116
  147.2 4.4 convolution_convert_fusion
  152.2 5.3 all-gather.12.cloned.1.call-done
  157.5 10.1 %copy.33 = bf16[256,8,2,1024]{3,1,2,0:T(8,128)(2,1)} copy(bf16[256,8,2,1024]{3,2,1,0:T(2,128)(2,1)} %bitcast.106) | data formatting | bytes 16777216
  167.6 145.8 %all-gather.16.cloned.1.call-done = bf16[4096,2048]{1,0:T(8,128)(2,1)} async-done(((bf16[1024,2048]{1,0:T(8,128)(2,1)}), bf16[4096,2048]{1,0:T(8,128)(2,1)}) %all-gather.16.cloned.1.call-update) | async-done | bytes 16777232 | tf_op jit(solution)/shard_map/all_gather | solution.py:15
  313.4 12.3 %reduce_sum.76 = bf16[1024,2048]{1,0:T(8,128)(2,1)} reduce(bf16[4,1024,2048]{2,1,0:T(8,128)(2,1)} %bitcast.104, bf16[]{:T(256)} %constant.60.clone.1), dimensions={0}, to_apply=%region_5.7 | reduce | flops 6291456 | bytes 20971522 | tf_op jit(solution)/shard_map/reduce_sum | solution.py:15
  325.7 5.1 fusion.48
  335.1 11.0 %fusion.96 = f32[1024,2048]{1,0:T(8,128)} fusion(bf16[1024,2048]{1,0:T(8,128)(2,1)S(1)} %bitcast.108, bf16[2048,2048]{1,0:T(8,128)(2,1)S(1)} %bitcast.107), kind=kOutput, calls=%fused_computation.117 | convolution fusion | flops 8589934592 | bytes 20971520 | tf_op jit(solution)/shard_map/dot_general | solution.py:126
  346.1 16.4 %all-gather.14.cloned.1.call-done = bf16[1024,2048]{0,1:T(8,128)(2,1)} async-done(((bf16[1024,64]{0,1:T(8,128)(2,1)}), bf16[1024,2048]{0,1:T(8,128)(2,1)}) %all-gather.14.cloned.1.call-update) | async-done | bytes 4194320 | tf_op jit(solution)/shard_map/all_gather | solution.py:134
  362.5 11.1 %convolution_convert_fusion.1 = bf16[1024,2048]{1,0:T(8,128)(2,1)} fusion(bf16[1024,2048]{0,1:T(8,128)(2,1)} %all-gather.14.cloned.1.call-done, f32[1024,2048]{1,0:T(8,128)} %fusion.96), kind=kOutput, calls=%fused_computation.61 | convolution fusion | flops 4303355904 | bytes 16777216 | tf_op jit(solution)/shard_map/dot_general | solution.py:132
  375.6 90.7 %all-reduce.3.cloned.1.call-done = bf16[2,512,2048]{2,1,0:T(8,128)(2,1)} async-done(((bf16[2,512,2048]{2,1,0:T(8,128)(2,1)}), bf16[2,512,2048]{2,1,0:T(8,128)(2,1)}) %all-reduce.3.cloned.1.call-update) | async-done | bytes 4194320 | tf_op jit(solution)/shard_map/psum | solution.py:137
  466.3 6.3 fusion.52
  475.0 24.8 %all-gather.1 = bf16[32,2,2048]{2,1,0:T(2,128)(2,1)S(1)} all-gather(bf16[1,2,2048]{2,1,0:T(2,128)(2,1)S(1)} %bitcast.114), channel_id=1, replica_groups=mesh['req'=32,'mlp'=4] {'req'}, dimensions={0}, use_global_device_ids=true | all-gather | bytes 270336 | tf_op jit(solution)/shard_map/all_gather | solution.py:149
  502.0 64.5 %pmax.7 = f32[64]{0:T(128)S(1)} all-reduce(f32[64]{0:T(128)S(1)} %convolution_reduce_fusion), channel_id=1, replica_groups=mesh['req'=32,'mlp'=4] {'req','mlp'}, use_global_device_ids=true, to_apply=%region_12.14 | all-reduce | flops 64 | bytes 512 | tf_op jit(solution)/shard_map/pmax | solution.py:158
  566.5 64.6 %all-reduce = f32[64]{0:T(128)S(1)} all-reduce(f32[64]{0:T(128)S(1)} %sqrt_dynamic-update-slice_fusion), channel_id=1, replica_groups=mesh['req'=32,'mlp'=4] {'req'}, use_global_device_ids=true, to_apply=%add | all-reduce | flops 64 | bytes 512
  (87 shorter events, 37.2 us)
Async XLA Ops:
  7.2 140.0 %copy-start = (bf16[512,2048]{1,0:T(8,128)(2,1)S(1)}, bf16[512,2048]{1,0:T(8,128)(2,1)}, u32[]{:S(2)}) copy-start(bf16[512,2048]{1,0:T(8,128)(2,1)} %param.28) | copy-start | bytes 6291460
  7.2 48.2 %all-gather.10.cloned.1.call-start = ((), (), s32[]{:S(2)}) async-start(), calls=%async_computation.1 | async-start | bytes 1081344 | tf_op jit(solution)/shard_map/all_gather | solution.py:77
  7.9 95.1 %all-gather.8.cloned.1.call-start = ((), (), s32[]{:S(2)}) async-start(), calls=%async_computation | async-start | bytes 4325376 | tf_op jit(solution)/shard_map/all_gather | solution.py:76
  8.7 148.8 %all-gather.12.cloned.1.call-start = ((), (), s32[]{:S(2)}) async-start(), calls=%async_computation.2 | async-start | bytes 8650752 | tf_op jit(solution)/shard_map/all_gather | solution.py:125
  9.4 304.0 %all-gather.16.cloned.1.call-start = ((), (), s32[]{:S(2)}) async-start(), calls=%async_computation.5 | async-start | bytes 20971520 | tf_op jit(solution)/shard_map/all_gather | solution.py:15
  18.3 3.4 copy-start.5
  18.3 3.4 copy-start.14
  30.8 3.3 copy-start.10
  30.8 3.4 copy-start.13
  30.8 3.5 copy-start.2
  30.8 4.2 copy-start.3
  30.8 4.9 copy-start.4
  151.6 210.9 %all-gather.14.cloned.1.call-start = ((), (), s32[]{:S(2)}) async-start(), calls=%async_computation.3 | async-start | bytes 4325376 | tf_op jit(solution)/shard_map/all_gather | solution.py:134
  152.2 314.1 %all-reduce.3.cloned.1.call-start = ((), (), s32[]{:S(2)}) async-start(), calls=%async_computation.4 | async-start | bytes 8388608 | tf_op jit(solution)/shard_map/psum | solution.py:137
  325.7 5.1 copy-start.6
  325.7 6.0 copy-start.7
  325.7 6.0 copy-start.11
  331.7 3.4 copy-start.9
  373.6 0.7 copy-start.15
  472.6 2.1 copy-start.8
  472.6 2.3 copy-start.12
  472.6 159.1 %copy-start.1 = (bf16[512,2048]{1,0:T(8,128)(2,1)S(1)}, bf16[512,2048]{1,0:T(8,128)(2,1)}, u32[]{:S(2)}) copy-start(bf16[512,2048]{1,0:T(8,128)(2,1)} %param.28) | copy-start | bytes 6291460
Sparse Core Ops, SparseCore 0:
  10.3 45.0 all-gather.9
  57.7 45.2 all-gather.7
  105.3 52.1 all-gather.11
  159.6 153.7 all-gather.15
  315.5 46.8 all-gather.13
  373.8 92.4 all-reduce.2
